TPU v7x, 32 devices: a whole 2x2x4 slice. The times are simulated.
32 devices in a mesh: grp: 2 (over x), tm: 16 (over z, y, core).
Axes of the slice: x: 2, y: 2, z: 4, core: 2. Of those that a mesh axis runs over, the one named last changes fastest.
Arguments:
- frames_in: bfloat16 [16384, 1536], P(('grp', 'tm')), parts along dimension 0, may hold values from -6 to 6
- frame_time: int32 [64], P('grp'), parts along dimension 0, may hold values from 0 to 31, each once
- norm_gain: float32 [1536], replicated, may hold values from 0.25 to 1.75
- w_query: bfloat16 [1536, 768], replicated, may hold values from -2 to 2
- w_key: bfloat16 [1536, 768], replicated, may hold values from -2 to 2
- w_value: bfloat16 [1536, 768], replicated, may hold values from -0.15625 to 0.15625
- w_output: bfloat16 [768, 1536], replicated, may hold values from -0.21875 to 0.21875
Outputs:
- attended: bfloat16 [16384, 1536], P(('grp', 'tm')), parts along dimension 0
There are 2 independent parts, one for each index of `grp`. A program takes and returns all parts, laid end to end along the dimension named above; an argument that names none is the same for every part. Nothing has to cross between parts.
Inputs may be any that keep to these rules, and one draw needn't show every extreme that they name: `frame_time`: each of 0 to 31 stands once.
All inputs are finite; a program needn't handle non-finite values.
Results may differ from a plain program's by a relative error of at most 0.004.
The roundings to bfloat16 on the way count: a program that leaves them out, or rounds other values in their place, can miss the bound.
Values may be sent and summed in bfloat16 or wider, within the bound.
A program may use at most 128 MiB of HBM per device.

v0:
```python
import jax
import jax.numpy as jnp
from jax import lax
from jax.sharding import PartitionSpec as P

HEADS = 6
HD = 128
HH = 16
WW = 16
WIN = 8
POOL = 4


def normed_rows(frames_in, norm_gain):
    values_f = frames_in.astype(jnp.float32)
    scale = lax.rsqrt(jnp.mean(values_f * values_f, axis=-1, keepdims=True) + 1e-06)
    return (values_f * scale * norm_gain).astype(jnp.bfloat16)


def to_windows(array, count):
    shaped = array.reshape(count, HH // WIN, WIN, WW // WIN, WIN, HEADS, HD)
    shaped = shaped.transpose(0, 1, 3, 2, 4, 5, 6)
    return shaped.reshape(count, HH // WIN * (WW // WIN), WIN * WIN, HEADS, HD)


def from_windows(array, count):
    shaped = array.reshape(count, HH // WIN, WW // WIN, WIN, WIN, HEADS * HD)
    shaped = shaped.transpose(0, 1, 3, 2, 4, 5)
    return shaped.reshape(count * HH * WW, HEADS * HD)


def pooled(array, count):
    pool_rows = HH // POOL * (WW // POOL)
    shaped = array.reshape(count, HH // POOL, POOL, WW // POOL, POOL, HEADS * HD).astype(
        jnp.float32
    )
    return jnp.mean(shaped, axis=(2, 4)).reshape(count * pool_rows, HEADS * HD).astype(jnp.bfloat16)


def on_device(frames_in, frame_time, norm_gain, w_query, w_key, w_value, w_output):
    count = frames_in.shape[0] // (HH * WW)
    pool_rows = HH // POOL * (WW // POOL)
    all_frames = frame_time.shape[0]
    normed = normed_rows(frames_in, norm_gain)
    query = jnp.dot(normed, w_query, preferred_element_type=jnp.float32).astype(jnp.bfloat16)
    keys = jnp.dot(normed, w_key, preferred_element_type=jnp.float32).astype(jnp.bfloat16)
    values = jnp.dot(normed, w_value, preferred_element_type=jnp.float32).astype(jnp.bfloat16)
    pooled_keys = pooled(keys, count)
    pooled_values = pooled(values, count)
    own_time = lax.dynamic_slice_in_dim(frame_time, lax.axis_index("tm") * count, count)
    query_win = to_windows(query, count)
    factor = 1.0 / HD**0.5
    local_s = (
        jnp.einsum(
            "fnqhd,fnkhd->fnhqk",
            query_win,
            to_windows(keys, count),
            preferred_element_type=jnp.float32,
        )
        * factor
    )
    top = jnp.max(local_s, -1)
    local_w = jnp.exp(local_s - top[..., None])
    local_acc = jnp.einsum(
        "fnhqk,fnkhd->fnhqd",
        local_w.astype(jnp.bfloat16),
        to_windows(values, count),
        preferred_element_type=jnp.float32,
    )
    whole_keys, whole_values = (
        lax.all_gather(pooled_keys, "tm", axis=0, tiled=True),
        lax.all_gather(pooled_values, "tm", axis=0, tiled=True),
    )
    rows = whole_keys.shape[0]
    slot = jnp.arange(rows, dtype=jnp.int32) // pool_rows
    match = slot[:, None] == jnp.arange(all_frames, dtype=jnp.int32)[None, :]
    key_time = jnp.sum(jnp.where(match, frame_time[None, :], 0), axis=1)
    best = top
    total = jnp.sum(local_w, -1)
    acc = local_acc
    scores = (
        jnp.einsum(
            "fnqhd,khd->fnhqk",
            query_win,
            whole_keys.reshape(rows, HEADS, HD),
            preferred_element_type=jnp.float32,
        )
        * factor
    )
    valid = (key_time[None, :] < own_time[:, None])[:, None, None, None, :]
    scores = jnp.where(valid, scores, -1e30)
    new_best = jnp.maximum(best, jnp.max(scores, -1))
    keep = jnp.exp(best - new_best)
    weights = jnp.where(valid, jnp.exp(scores - new_best[..., None]), 0.0)
    total = total * keep + jnp.sum(weights, -1)
    acc = acc * keep[..., None] + jnp.einsum(
        "fnhqk,khd->fnhqd",
        weights.astype(jnp.bfloat16),
        whole_values.reshape(rows, HEADS, HD),
        preferred_element_type=jnp.float32,
    )
    final = (new_best, total, acc)
    best, total, acc = final
    mixed = (acc / total[..., None]).transpose(0, 1, 3, 2, 4).astype(jnp.bfloat16)
    mixed = from_windows(mixed, count)
    return jnp.dot(mixed, w_output, preferred_element_type=jnp.float32).astype(jnp.bfloat16)


def solution(mesh):
    placed = (P(("grp", "tm"), None), P("grp"), P(), P(), P(), P(), P())
    return jax.shard_map(
        on_device, mesh=mesh, in_specs=placed, out_specs=P(("grp", "tm"), None), check_vma=False
    )
```

profile of v0, /device:TPU:0, one launch (start us, length us, event | category | flops | bytes accessed | tf_op | source)
XLA Modules:
  0.0 85.4 jit_solution(2821864571280386767)
XLA Ops:
  0.0 0.0 copy-start
  0.0 0.9 %dynamic_slice.3 = s32[2]{0:T(128)S(1)} dynamic-slice(s32[32]{0:T(128)} %param.8, s32[]{:T(128)S(6)} %select_n.25), dynamic_slice_sizes={2} | dynamic-slice | bytes 20 | tf_op jit(solution)/shard_map/dynamic_slice | solution.py:50
  0.9 0.7 select_reduce_fusion
  1.6 0.1 broadcast_compare_fusion
  1.7 1.8 %fusion.3 = f32[512]{0:T(512)S(1)} fusion(bf16[512,1536]{1,0:T(8,128)(2,1)} %param.7), kind=kLoop, calls=%fused_computation.7 | loop fusion | flops 2358784 | bytes 1574912 | tf_op jit(solution)/shard_map/reduce_sum | solution.py:16
  3.5 3.6 %convolution_convert_fusion.2 = bf16[512,768]{1,0:T(8,128)(2,1)S(1)} fusion(bf16[1536,768]{1,0:T(8,128)(2,1)} %param.11, bf16[512,1536]{1,0:T(8,128)(2,1)} %param.7, f32[1536]{0:T(1024)} %param.9, f32[512]{0:T(512)S(1)} %add_rsqrt_fusion), kind=kOutput, calls=%fused_computation.20 | convolution fusion | flops 1211498496 | bytes 4726784 | tf_op jit(solution)/shard_map/dot_general | solution.py:46
  7.1 0.0 copy-start.3
  7.1 1.5 %reshape.124 = f32[2,4,4,4,4,768]{5,4,3,2,1,0:T(4,128)} reshape(bf16[512,768]{1,0:T(8,128)(2,1)S(1)} %convolution_convert_fusion.2) | data formatting | bytes 2359296 | tf_op jit(solution)/shard_map/convert_element_type | solution.py:34
  8.6 0.0 copy-start.9
  8.6 1.9 %reduce_sum.60 = f32[2,4,4,768]{3,2,1,0:T(4,128)S(1)} reduce(f32[2,4,4,4,4,768]{5,4,3,2,1,0:T(4,128)} %reshape.124, f32[]{:T(128)} %constant.15.clone.1), dimensions={2,4}, to_apply=%region_3.0 | reduce | flops 368640 | bytes 1671172 | tf_op jit(solution)/shard_map/reduce_sum | solution.py:37
  10.6 0.0 copy-done.3
  10.6 26.7 %all_gather.6 = bf16[512,768]{1,0:T(8,128)(2,1)} all-gather(bf16[32,768]{1,0:T(8,128)(2,1)S(1)} %convert_element_type.60), channel_id=1, replica_groups=mesh['grp'=2,'tm'=16] {'tm'}, dimensions={0}, use_global_device_ids=true | all-gather | bytes 835584 | tf_op jit(solution)/shard_map/all_gather | solution.py:71
  37.3 1.4 %copy.75 = bf16[512,768]{0,1:T(8,128)(2,1)S(1)} copy(bf16[512,768]{1,0:T(8,128)(2,1)} %all_gather.6) | data formatting | bytes 1572864 | tf_op jit(solution)/shard_map/all_gather | solution.py:71
  38.8 0.0 copy-done.9
  38.8 3.6 %convolution_convert_fusion.3 = bf16[512,768]{1,0:T(8,128)(2,1)S(1)} fusion(bf16[1536,768]{1,0:T(8,128)(2,1)} %param.10, bf16[512,1536]{1,0:T(8,128)(2,1)} %param.7, f32[1536]{0:T(1024)S(1)} %copy-done.9, f32[512]{0:T(512)S(1)} %add_rsqrt_fusion), kind=kOutput, calls=%fused_computation.21 | convolution fusion | flops 1211498496 | bytes 4726784 | tf_op jit(solution)/shard_map/dot_general | solution.py:45
  42.4 0.2 copy.70
  42.6 0.0 copy-start.4
  42.6 1.1 %fusion = (f32[2,4,6,64]{3,1,0,2:T(4,128)S(1)}, f32[6,512,2,4,64]{1,4,3,2,0:T(8,128)S(1)}) fusion(pred[2,512]{1,0:T(4,128)(4,1)S(1)} %broadcast_compare_fusion, bf16[512,6,128,1,1]{0,2,4,3,1:T(8,128)(2,1)S(1)} %bitcast.70, bf16[2,4,64,6,128]{4,2,1,0,3:T(8,128)(2,1)S(1)} %bitcast.68), kind=kOutput, calls=%fused_computation.2 | convolution fusion | flops 407368704 | bytes 7877632 | tf_op jit(solution)/shard_map/fnqhd,khd->fnhqk/dot_general | solution.py:82
  43.7 0.0 copy-done.4
  43.7 0.2 copy.71
  43.9 0.6 fusion.23
  44.5 0.0 copy-start.1
  44.6 0.0 copy-start.7
  44.6 0.0 copy-start.8
  44.6 3.1 %fusion.1 = (f32[2,4,6,64]{3,1,0,2:T(4,128)S(1)}, bf16[2,4,6,64,512]{4,3,1,0,2:T(8,128)(2,1)}) fusion(f32[6,512,2,4,64]{1,4,3,2,0:T(8,128)S(1)} %get-tuple-element.12, f32[2,4,6,64]{3,1,0,2:T(4,128)S(1)} %copy.80, pred[2,512]{1,0:T(4,128)(4,1)S(1)} %broadcast_compare_fusion), kind=kLoop, calls=%fused_computation.3 | loop fusion | flops 9434112 | bytes 9462784 | tf_op jit(solution)/shard_map/reduce_sum | solution.py:95
  47.7 0.0 copy-done.1
  47.7 0.4 fusion.10
  48.1 0.0 copy-done.7
  48.2 0.2 copy-done.8
  48.4 1.5 %convolution_convert_fusion.1 = bf16[512,768]{1,0:T(8,128)(2,1)S(1)} fusion(bf16[1536,768]{1,0:T(8,128)(2,1)S(1)} %copy-done.8, bf16[512,1536]{1,0:T(8,128)(2,1)S(1)} %copy-done.7, f32[1536]{0:T(1024)S(1)} %copy-done.9, f32[512]{0:T(512)S(1)} %add_rsqrt_fusion), kind=kOutput, calls=%fused_computation.19 | convolution fusion | flops 1211498496 | bytes 4726784 | tf_op jit(solution)/shard_map/dot_general | solution.py:47
  49.9 0.0 copy-start.5
  49.9 1.5 %reshape.125 = f32[2,4,4,4,4,768]{5,4,3,2,1,0:T(4,128)} reshape(bf16[512,768]{1,0:T(8,128)(2,1)S(1)} %convolution_convert_fusion.1) | data formatting | bytes 2359296 | tf_op jit(solution)/shard_map/convert_element_type | solution.py:34
  51.4 1.9 %reduce_sum.61 = f32[2,4,4,768]{3,2,1,0:T(4,128)S(1)} reduce(f32[2,4,4,4,4,768]{5,4,3,2,1,0:T(4,128)} %reshape.125, f32[]{:T(128)} %constant.15.clone.1), dimensions={2,4}, to_apply=%region_5.6 | reduce | flops 368640 | bytes 1671172 | tf_op jit(solution)/shard_map/reduce_sum | solution.py:37
  53.3 0.0 copy-done.5
  53.4 19.8 %all_gather.7 = bf16[512,768]{1,0:T(8,128)(2,1)S(1)} all-gather(bf16[32,768]{1,0:T(8,128)(2,1)S(1)} %convert_element_type.64), channel_id=1, replica_groups=mesh['grp'=2,'tm'=16] {'tm'}, dimensions={0}, use_global_device_ids=true | all-gather | bytes 835584 | tf_op jit(solution)/shard_map/all_gather | solution.py:72
  73.1 1.2 %copy.78 = bf16[512,768]{0,1:T(8,128)(2,1)} copy(bf16[512,768]{1,0:T(8,128)(2,1)S(1)} %all_gather.7) | data formatting | bytes 1572864 | tf_op jit(solution)/shard_map/all_gather | solution.py:72
  74.3 0.0 copy-start.6
  74.3 0.0 copy-start.2
  74.3 3.3 %fusion.6 = f32[6,128,2,4,64]{1,4,0,3,2:T(8,128)S(1)} fusion(bf16[512,6,128,1,1]{0,2,1,4,3:T(8,128)(2,1)} %bitcast.76, bf16[2,4,6,64,512]{4,3,1,0,2:T(8,128)(2,1)} %get-tuple-element.8), kind=kOutput, calls=%fused_computation.10 | convolution fusion | flops 402653184 | bytes 5505024 | tf_op jit(solution)/shard_map/fnhqk,khd->fnhqd/dot_general | solution.py:96
  77.6 0.0 copy-done.6
  77.6 0.2 copy.73
  77.8 0.0 copy-done.2
  77.8 1.5 %fusion.9 = bf16[2,4,64,6,128]{4,2,3,1,0:T(8,128)(2,1)S(1)} fusion(f32[6,128,2,4,64]{1,4,0,3,2:T(8,128)S(1)} %fusion.6, bf16[2,4,64,6,128]{4,2,3,1,0:T(8,128)(2,1)S(1)} %bitcast.75, f32[2,4,6,64,64]{3,4,2,1,0:T(8,128)S(1)} %copy-done.2, f32[2,4,64,6]{2,3,1,0:T(8,128)S(1)} %get-tuple-element.5, f32[2,4,64,6]{2,3,1,0:T(8,128)S(1)} %get-tuple-element.6, ...), kind=kOutput, calls=%fused_computation.15 | convolution fusion | flops 52297728 | bytes 3969024 | tf_op jit(solution)/shard_map/fnhqk,fnkhd->fnhqd/dot_general | solution.py:64
  79.3 0.6 copy.84
  79.8 1.8 %reshape.122 = bf16[2,2,2,8,8,768]{5,4,3,2,1,0:T(8,128)(2,1)} reshape(bf16[2,4,64,6,128]{4,3,2,1,0:T(8,128)(2,1)S(1)} %copy.84) | data formatting | bytes 1572864 | tf_op jit(solution)/shard_map/reshape | solution.py:27
  81.6 1.2 %copy.85 = bf16[2,2,8,2,8,768]{5,4,3,2,1,0:T(8,128)(2,1)S(1)} copy(bf16[2,2,8,2,8,768]{5,4,2,3,1,0:T(8,128)(2,1)} %bitcast.71) | data formatting | bytes 1572864 | tf_op jit(solution)/shard_map/transpose | solution.py:28
  82.8 0.0 copy-done
  82.8 2.5 %convolution_convert_fusion = bf16[512,1536]{1,0:T(8,128)(2,1)} fusion(bf16[512,768]{1,0:T(8,128)(2,1)S(1)} %bitcast.77, bf16[768,1536]{1,0:T(8,128)(2,1)S(1)} %copy-done), kind=kOutput, calls=%fused_computation.12 | convolution fusion | flops 1208745984 | bytes 4718592 | tf_op jit(solution)/shard_map/dot_general | solution.py:106
  (9 shorter events, 0.1 us)
Async XLA Ops:
  0.0 82.8 %copy-start = (bf16[768,1536]{1,0:T(8,128)(2,1)S(1)}, bf16[768,1536]{1,0:T(8,128)(2,1)}, u32[]{:S(2)}) copy-start(bf16[768,1536]{1,0:T(8,128)(2,1)} %param.13) | copy-start | bytes 7077892
  7.1 3.5 %copy-start.3 = (bf16[512,768]{1,0:T(8,128)(2,1)}, bf16[512,768]{1,0:T(8,128)(2,1)S(1)}, u32[]{:S(2)}) copy-start(bf16[512,768]{1,0:T(8,128)(2,1)S(1)} %convolution_convert_fusion.2) | copy-start | bytes 2359300
  8.6 30.1 %copy-start.9 = (f32[1536]{0:T(1024)S(1)}, f32[1536]{0:T(1024)}, u32[]{:S(2)}) copy-start(f32[1536]{0:T(1024)} %param.9) | copy-start | bytes 18436
  42.6 1.1 %copy-start.4 = (bf16[512,768]{1,0:T(8,128)(2,1)S(1)}, bf16[512,768]{1,0:T(8,128)(2,1)}, u32[]{:S(2)}) copy-start(bf16[512,768]{1,0:T(8,128)(2,1)} %copy-done.3) | copy-start | bytes 2359300
  44.5 3.2 %copy-start.1 = (f32[2,4,6,64,64]{3,4,2,1,0:T(8,128)}, f32[2,4,6,64,64]{3,4,2,1,0:T(8,128)S(1)}, u32[]{:S(2)}) copy-start(f32[2,4,6,64,64]{3,4,2,1,0:T(8,128)S(1)} %get-tuple-element.10) | copy-start | bytes 2359300
  44.6 3.6 %copy-start.7 = (bf16[512,1536]{1,0:T(8,128)(2,1)S(1)}, bf16[512,1536]{1,0:T(8,128)(2,1)}, u32[]{:S(2)}) copy-start(bf16[512,1536]{1,0:T(8,128)(2,1)} %param.7) | copy-start | bytes 4718596
  44.6 3.8 %copy-start.8 = (bf16[1536,768]{1,0:T(8,128)(2,1)S(1)}, bf16[1536,768]{1,0:T(8,128)(2,1)}, u32[]{:S(2)}) copy-start(bf16[1536,768]{1,0:T(8,128)(2,1)} %param.12) | copy-start | bytes 7077892
  49.9 3.5 %copy-start.5 = (bf16[512,768]{1,0:T(8,128)(2,1)}, bf16[512,768]{1,0:T(8,128)(2,1)S(1)}, u32[]{:S(2)}) copy-start(bf16[512,768]{1,0:T(8,128)(2,1)S(1)} %convolution_convert_fusion.1) | copy-start | bytes 2359300
  74.3 3.3 %copy-start.6 = (bf16[512,768]{1,0:T(8,128)(2,1)S(1)}, bf16[512,768]{1,0:T(8,128)(2,1)}, u32[]{:S(2)}) copy-start(bf16[512,768]{1,0:T(8,128)(2,1)} %copy-done.5) | copy-start | bytes 2359300
  74.3 3.5 %copy-start.2 = (f32[2,4,6,64,64]{3,4,2,1,0:T(8,128)S(1)}, f32[2,4,6,64,64]{3,4,2,1,0:T(8,128)}, u32[]{:S(2)}) copy-start(f32[2,4,6,64,64]{3,4,2,1,0:T(8,128)} %copy-done.1) | copy-start | bytes 2359300
where the time goes:
time: 85.7 us; the launch traced here: 85.4 us
  blocking collectives  46.5 us (54%)
  matrix products  17.6 us (21%)
  local copies, waits for them, and re-layouts  11 us (13%)
  other arithmetic  9.99 us (12%)
    all_gather x1, blocking collectives, on_device(): lax.all_gather(pooled_keys, 'tm', axis=0, tiled=True)  26.7 us
    all_gather x1, blocking collectives, on_device(): lax.all_gather(pooled_values, 'tm', axis=0, tiled=True)  19.8 us
    reduce_sum x2, other arithmetic, pooled(): jnp.mean(shaped, axis=(2, 4)).reshape(count * pool_rows, HEADS * HD)  3.78 us
    dot_general x1, matrix products, on_device(): jnp.dot(normed, w_key, preferred_element_type=jnp.float32)  3.6 us
    dot_general x1, matrix products, on_device(): jnp.dot(normed, w_query, preferred_element_type=jnp.float32)  3.58 us
    dot_general x1, matrix products, on_device(): jnp.einsum('fnhqk,khd->fnhqd', weights.astype(jnp.bfloat16), whole_values...  3.25 us
    reduce_sum x1, other arithmetic, on_device(): total = total * keep + jnp.sum(weights, -1)  3.13 us
    convert_element_type x2, local copies, waits for them, and re-layouts, pooled(): array.reshape(count, HH // POOL, POOL, WW // POOL, POOL, HEADS * HD)  3.03 us

commit v1 on v0

--- a/solution.py
+++ b/solution.py
@@ -9,6 +9,16 @@
 WW = 16
 WIN = 8
 POOL = 4
+
+
+def gather_around(x, axis, dim):
+    ways, here, step = (lax.axis_size(axis), lax.axis_index(axis), x.shape[dim])
+    lengths = [n * ways if d == dim else n for d, n in enumerate(x.shape)]
+    full = lax.dynamic_update_slice_in_dim(jnp.zeros(lengths, x.dtype), x, here * step, axis=dim)
+    for far in range(1, ways):
+        x = lax.ppermute(x, axis, [(d, (d + 1) % ways) for d in range(ways)])
+        full = lax.dynamic_update_slice_in_dim(full, x, (here - far) % ways * step, axis=dim)
+    return full
 
 
 def normed_rows(frames_in, norm_gain):
@@ -69,7 +79,7 @@
     )
     whole_keys, whole_values = (
         lax.all_gather(pooled_keys, "tm", axis=0, tiled=True),
-        lax.all_gather(pooled_values, "tm", axis=0, tiled=True),
+        gather_around(pooled_values, "tm", 0),
     )
     rows = whole_keys.shape[0]
     slot = jnp.arange(rows, dtype=jnp.int32) // pool_rows

time: 85.7 us -> 172 us (2.01)
  waiting for transfers between devices: 0 us -> 58.5 us
  local copies, waits for them, and re-layouts: 11 us -> 59.4 us
  blocking collectives: 46.5 us -> 21.5 us
  matrix products: 17.6 us -> 20.7 us
    ppermute x0 -> x15, waiting for transfers between devices: none -> 58.5 us  [gather_around(): x = lax.ppermute(x, axis, [(d, (d + 1) % ways) for d in range(ways)])]
    dynamic_update_slice x0 -> x16, local copies, waits for them, and re-layouts: none -> 41 us  [the longest x15 38.8 us: gather_around(): lax.dynamic_update_slice_in_dim(full, x, (here - far) % ways * step, axis...]
    all_gather x1 -> x0, blocking collectives: 19.8 us -> none  [on_device(): lax.all_gather(pooled_values, 'tm', axis=0, tiled=True)]
    ppermute x0 -> x15, local copies, waits for them, and re-layouts: none -> 7.24 us  [gather_around(): x = lax.ppermute(x, axis, [(d, (d + 1) % ways) for d in range(ways)])]
    all_gather x1, blocking collectives: 26.7 us -> 21.5 us  [on_device(): lax.all_gather(pooled_keys, 'tm', axis=0, tiled=True)]
    dot_general x1, matrix products: 1.47 us -> 3.6 us  [on_device(): jnp.dot(normed, w_value, preferred_element_type=jnp.float32)]
  transfers between devices with their start and end apart: 0 -> 15, of which waited for: 0 -> 13; matrix products, arithmetic and copies ran while one was open for 0% -> 40% of each run, Pallas kernels for 0% -> 0%
where the time goes in v1:
time: 172 us
  local copies, waits for them, and re-layouts  59.4 us (35%)
  waiting for transfers between devices  58.5 us (34%)
  blocking collectives  21.5 us (12%)
  matrix products  20.7 us (12%)
  other arithmetic  10.1 us (6%)
    ppermute x15, waiting for transfers between devices, gather_around(): x = lax.ppermute(x, axis, [(d, (d + 1) % ways) for d in range(ways)])  58.5 us
    dynamic_update_slice x15, local copies, waits for them, and re-layouts, gather_around(): lax.dynamic_update_slice_in_dim(full, x, (here - far) % ways * step, axis...  38.8 us
    all_gather x1, blocking collectives, on_device(): lax.all_gather(pooled_keys, 'tm', axis=0, tiled=True)  21.5 us
    ppermute x15, local copies, waits for them, and re-layouts, gather_around(): x = lax.ppermute(x, axis, [(d, (d + 1) % ways) for d in range(ways)])  7.24 us
    dot_general x1, matrix products, on_device(): jnp.dot(normed, w_key, preferred_element_type=jnp.float32)  4.48 us
    reduce_sum x2, other arithmetic, pooled(): jnp.mean(shaped, axis=(2, 4)).reshape(count * pool_rows, HEADS * HD)  3.78 us
    dot_general x1, matrix products, on_device(): jnp.dot(normed, w_value, preferred_element_type=jnp.float32)  3.6 us
  transfers between devices with their start and end apart: 15, of which 13 were waited for; matrix products, arithmetic and copies ran while one was open for 40% of the time, Pallas kernels for 0%

profile of v1, /device:TPU:0, one launch (start us, length us, event | category | flops | bytes accessed | tf_op | source)
XLA Modules:
  0.0 171.6 jit_solution(8869464249306836666)
XLA Ops:
  0.0 1.9 %fusion.3 = f32[512]{0:T(512)S(1)} fusion(bf16[512,1536]{1,0:T(8,128)(2,1)} %param.7), kind=kLoop, calls=%fused_computation.7 | loop fusion | flops 2358784 | bytes 1574912 | tf_op jit(solution)/shard_map/reduce_sum | solution.py:26
  2.0 3.6 %convolution_convert_fusion.1 = bf16[512,768]{1,0:T(8,128)(2,1)S(1)} fusion(bf16[1536,768]{1,0:T(8,128)(2,1)} %param.12, bf16[512,1536]{1,0:T(8,128)(2,1)} %param.7, f32[1536]{0:T(1024)} %param.9, f32[512]{0:T(512)S(1)} %add_rsqrt_fusion), kind=kOutput, calls=%fused_computation.19 | convolution fusion | flops 1211498496 | bytes 4726784 | tf_op jit(solution)/shard_map/dot_general | solution.py:57
  5.6 1.5 reshape.125
  7.1 1.9 %reduce_sum.61 = f32[2,4,4,768]{3,2,1,0:T(4,128)S(1)} reduce(f32[2,4,4,4,4,768]{5,4,3,2,1,0:T(4,128)} %reshape.125, f32[]{:T(128)} %constant.126.clone.1), dimensions={2,4}, to_apply=%region_5.6 | reduce | flops 368640 | bytes 1671172 | tf_op jit(solution)/shard_map/reduce_sum | solution.py:47
  9.6 6.8 %collective-permute-done = bf16[32,768]{1,0:T(8,128)(2,1)S(1)} collective-permute-done((bf16[32,768]{1,0:T(8,128)(2,1)S(1)}, bf16[32,768]{1,0:T(8,128)(2,1)S(1)}, u32[]{:S(2)}, u32[]{:S(2)}) %collective-permute-start) | collective-permute-done | bytes 49184 | tf_op jit(solution)/shard_map/ppermute | solution.py:19
  16.4 4.5 %convolution_convert_fusion.2 = bf16[512,768]{1,0:T(8,128)(2,1)} fusion(bf16[1536,768]{1,0:T(8,128)(2,1)} %param.11, bf16[512,1536]{1,0:T(8,128)(2,1)} %param.7, f32[1536]{0:T(1024)S(1)} %copy-done.26, f32[512]{0:T(512)S(1)} %add_rsqrt_fusion), kind=kOutput, calls=%fused_computation.20 | convolution fusion | flops 1211498496 | bytes 4726784 | tf_op jit(solution)/shard_map/dot_general | solution.py:56
  20.9 1.7 %collective-permute-done.1 = bf16[32,768]{1,0:T(8,128)(2,1)S(1)} collective-permute-done((bf16[32,768]{1,0:T(8,128)(2,1)S(1)}, bf16[32,768]{1,0:T(8,128)(2,1)S(1)}, u32[]{:S(2)}, u32[]{:S(2)}) %collective-permute-start.1) | collective-permute-done | bytes 49184 | tf_op jit(solution)/shard_map/ppermute | solution.py:19
  22.6 2.4 %convolution_convert_fusion.3 = bf16[512,768]{1,0:T(8,128)(2,1)} fusion(bf16[1536,768]{1,0:T(8,128)(2,1)S(1)} %copy-done.25, bf16[512,1536]{1,0:T(8,128)(2,1)S(1)} %copy-done.5, f32[1536]{0:T(1024)S(1)} %copy-done.26, f32[512]{0:T(512)S(1)} %add_rsqrt_fusion), kind=kOutput, calls=%fused_computation.21 | convolution fusion | flops 1211498496 | bytes 4726784 | tf_op jit(solution)/shard_map/dot_general | solution.py:55
  25.0 1.5 reshape.124
  26.5 1.9 %reduce_sum.60 = f32[2,4,4,768]{3,2,1,0:T(4,128)S(1)} reduce(f32[2,4,4,4,4,768]{5,4,3,2,1,0:T(4,128)} %reshape.124, f32[]{:T(128)} %constant.126.clone.1), dimensions={2,4}, to_apply=%region_3.0 | reduce | flops 368640 | bytes 1671172 | tf_op jit(solution)/shard_map/reduce_sum | solution.py:47
  28.9 6.2 %collective-permute-done.3 = bf16[32,768]{1,0:T(8,128)(2,1)S(1)} collective-permute-done((bf16[32,768]{1,0:T(8,128)(2,1)S(1)}, bf16[32,768]{1,0:T(8,128)(2,1)S(1)}, u32[]{:S(2)}, u32[]{:S(2)}) %collective-permute-start.3) | collective-permute-done | bytes 49184 | tf_op jit(solution)/shard_map/ppermute | solution.py:19
  35.0 21.5 %all_gather.3 = bf16[512,768]{1,0:T(8,128)(2,1)} all-gather(bf16[32,768]{1,0:T(8,128)(2,1)S(1)} %convert_element_type.60), channel_id=1, replica_groups=mesh['grp'=2,'tm'=16] {'tm'}, dimensions={0}, use_global_device_ids=true | all-gather | bytes 835584 | tf_op jit(solution)/shard_map/all_gather | solution.py:81
  56.7 6.0 %collective-permute-done.5 = bf16[32,768]{1,0:T(8,128)(2,1)S(1)} collective-permute-done((bf16[32,768]{1,0:T(8,128)(2,1)S(1)}, bf16[32,768]{1,0:T(8,128)(2,1)S(1)}, u32[]{:S(2)}, u32[]{:S(2)}) %collective-permute-start.5) | collective-permute-done | bytes 49184 | tf_op jit(solution)/shard_map/ppermute | solution.py:19
  62.9 6.0 %collective-permute-done.6 = bf16[32,768]{1,0:T(8,128)(2,1)S(1)} collective-permute-done((bf16[32,768]{1,0:T(8,128)(2,1)S(1)}, bf16[32,768]{1,0:T(8,128)(2,1)S(1)}, u32[]{:S(2)}, u32[]{:S(2)}) %collective-permute-start.6) | collective-permute-done | bytes 49184 | tf_op jit(solution)/shard_map/ppermute | solution.py:19
  69.1 1.3 copy.115
  70.4 2.3 %copy.120 = bf16[512,768]{0,1:T(8,128)(2,1)} copy(bf16[512,768]{1,0:T(8,128)(2,1)} %all_gather.3) | data formatting | bytes 1572864 | tf_op jit(solution)/shard_map/all_gather | solution.py:81
  72.7 2.5 %collective-permute-done.7 = bf16[32,768]{1,0:T(8,128)(2,1)S(1)} collective-permute-done((bf16[32,768]{1,0:T(8,128)(2,1)S(1)}, bf16[32,768]{1,0:T(8,128)(2,1)S(1)}, u32[]{:S(2)}, u32[]{:S(2)}) %collective-permute-start.7) | collective-permute-done | bytes 49184 | tf_op jit(solution)/shard_map/ppermute | solution.py:19
  75.2 2.3 %fusion = (f32[2,4,6,64]{3,1,0,2:T(4,128)S(1)}, f32[6,512,2,4,64]{1,4,3,2,0:T(8,128)S(1)}) fusion(pred[2,512]{1,0:T(4,128)(4,1)S(1)} %broadcast_compare_fusion, bf16[512,6,128,1,1]{0,2,4,3,1:T(8,128)(2,1)} %bitcast.70, bf16[2,4,64,6,128]{4,2,1,0,3:T(8,128)(2,1)S(1)} %bitcast.68), kind=kOutput, calls=%fused_computation.2 | convolution fusion | flops 407368704 | bytes 7877632 | tf_op jit(solution)/shard_map/fnqhd,khd->fnhqk/dot_general | solution.py:92
  77.8 3.7 %collective-permute-done.8 = bf16[32,768]{1,0:T(8,128)(2,1)S(1)} collective-permute-done((bf16[32,768]{1,0:T(8,128)(2,1)S(1)}, bf16[32,768]{1,0:T(8,128)(2,1)S(1)}, u32[]{:S(2)}, u32[]{:S(2)}) %collective-permute-start.8) | collective-permute-done | bytes 49184 | tf_op jit(solution)/shard_map/ppermute | solution.py:19
  82.0 5.7 %collective-permute-done.9 = bf16[32,768]{1,0:T(8,128)(2,1)S(1)} collective-permute-done((bf16[32,768]{1,0:T(8,128)(2,1)S(1)}, bf16[32,768]{1,0:T(8,128)(2,1)S(1)}, u32[]{:S(2)}, u32[]{:S(2)}) %collective-permute-start.9) | collective-permute-done | bytes 49184 | tf_op jit(solution)/shard_map/ppermute | solution.py:19
  87.7 6.2 %collective-permute-done.10 = bf16[32,768]{1,0:T(8,128)(2,1)S(1)} collective-permute-done((bf16[32,768]{1,0:T(8,128)(2,1)S(1)}, bf16[32,768]{1,0:T(8,128)(2,1)S(1)}, u32[]{:S(2)}, u32[]{:S(2)}) %collective-permute-start.10) | collective-permute-done | bytes 49184 | tf_op jit(solution)/shard_map/ppermute | solution.py:19
  93.9 3.1 %fusion.1 = (f32[2,4,6,64]{3,1,0,2:T(4,128)S(1)}, bf16[2,4,6,64,512]{4,3,1,0,2:T(8,128)(2,1)}) fusion(f32[6,512,2,4,64]{1,4,3,2,0:T(8,128)S(1)} %get-tuple-element.12, f32[2,4,6,64]{3,1,0,2:T(4,128)S(1)} %copy.140, pred[2,512]{1,0:T(4,128)(4,1)S(1)} %broadcast_compare_fusion), kind=kLoop, calls=%fused_computation.3 | loop fusion | flops 9434112 | bytes 9462784 | tf_op jit(solution)/shard_map/reduce_sum | solution.py:105
  97.2 2.8 %collective-permute-done.11 = bf16[32,768]{1,0:T(8,128)(2,1)S(1)} collective-permute-done((bf16[32,768]{1,0:T(8,128)(2,1)S(1)}, bf16[32,768]{1,0:T(8,128)(2,1)S(1)}, u32[]{:S(2)}, u32[]{:S(2)}) %collective-permute-start.11) | collective-permute-done | bytes 49184 | tf_op jit(solution)/shard_map/ppermute | solution.py:19
  100.1 1.6 fusion.14
  101.7 4.6 %collective-permute-done.12 = bf16[32,768]{1,0:T(8,128)(2,1)S(1)} collective-permute-done((bf16[32,768]{1,0:T(8,128)(2,1)S(1)}, bf16[32,768]{1,0:T(8,128)(2,1)S(1)}, u32[]{:S(2)}, u32[]{:S(2)}) %collective-permute-start.12) | collective-permute-done | bytes 49184 | tf_op jit(solution)/shard_map/ppermute | solution.py:19
  106.7 5.9 %collective-permute-done.13 = bf16[32,768]{1,0:T(8,128)(2,1)} collective-permute-done((bf16[32,768]{1,0:T(8,128)(2,1)S(1)}, bf16[32,768]{1,0:T(8,128)(2,1)}, u32[]{:S(2)}, u32[]{:S(2)}) %collective-permute-start.13) | collective-permute-done | bytes 49184 | tf_op jit(solution)/shard_map/ppermute | solution.py:19
  113.6 2.2 %dynamic_update_slice.48 = bf16[512,768]{0,1:T(8,128)(2,1)S(1)} dynamic-update-slice(bf16[512,768]{0,1:T(8,128)(2,1)S(1)} %broadcast_in_dim.49, bf16[32,768]{0,1:T(8,128)(2,1)S(1)} %copy.123, s32[]{:T(128)S(6)} %select_n.138, s32[]{:T(128)} %constant.133.clone.1) | dynamic-update-slice | bytes 98308 | tf_op jit(solution)/shard_map/dynamic_update_slice | solution.py:17
  116.0 2.4 %dynamic_update_slice.49 = bf16[512,768]{0,1:T(8,128)(2,1)S(1)} dynamic-update-slice(bf16[512,768]{0,1:T(8,128)(2,1)S(1)} %dynamic_update_slice.48, bf16[32,768]{0,1:T(8,128)(2,1)S(1)} %copy.124, s32[]{:T(128)S(6)} %select_n.140, s32[]{:T(128)} %constant.133.clone.1) | dynamic-update-slice | bytes 98308 | tf_op jit(solution)/shard_map/dynamic_update_slice | solution.py:20
  118.6 2.4 %dynamic_update_slice.50 = bf16[512,768]{0,1:T(8,128)(2,1)S(1)} dynamic-update-slice(bf16[512,768]{0,1:T(8,128)(2,1)S(1)} %dynamic_update_slice.49, bf16[32,768]{0,1:T(8,128)(2,1)S(1)} %copy.125, s32[]{:T(128)S(6)} %select_n.142, s32[]{:T(128)} %constant.133.clone.1) | dynamic-update-slice | bytes 98308 | tf_op jit(solution)/shard_map/dynamic_update_slice | solution.py:20
  121.1 2.4 %dynamic_update_slice.51 = bf16[512,768]{0,1:T(8,128)(2,1)S(1)} dynamic-update-slice(bf16[512,768]{0,1:T(8,128)(2,1)S(1)} %dynamic_update_slice.50, bf16[32,768]{0,1:T(8,128)(2,1)S(1)} %copy.126, s32[]{:T(128)S(6)} %select_n.144, s32[]{:T(128)} %constant.133.clone.1) | dynamic-update-slice | bytes 98308 | tf_op jit(solution)/shard_map/dynamic_update_slice | solution.py:20
  124.5 1.6 dynamic_update_slice.52
  126.1 1.0 copy.128
  127.1 2.9 %dynamic_update_slice.53 = bf16[512,768]{0,1:T(8,128)(2,1)S(1)} dynamic-update-slice(bf16[512,768]{0,1:T(8,128)(2,1)S(1)} %dynamic_update_slice.52, bf16[32,768]{0,1:T(8,128)(2,1)S(1)} %copy.128, s32[]{:T(128)S(6)} %select_n.148, s32[]{:T(128)} %constant.133.clone.1) | dynamic-update-slice | bytes 98308 | tf_op jit(solution)/shard_map/dynamic_update_slice | solution.py:20
  129.9 1.0 copy.129
  130.9 2.9 %dynamic_update_slice.54 = bf16[512,768]{0,1:T(8,128)(2,1)S(1)} dynamic-update-slice(bf16[512,768]{0,1:T(8,128)(2,1)S(1)} %dynamic_update_slice.53, bf16[32,768]{0,1:T(8,128)(2,1)S(1)} %copy.129, s32[]{:T(128)S(6)} %select_n.150, s32[]{:T(128)} %constant.133.clone.1) | dynamic-update-slice | bytes 98308 | tf_op jit(solution)/shard_map/dynamic_update_slice | solution.py:20
  134.0 2.9 %dynamic_update_slice.55 = bf16[512,768]{0,1:T(8,128)(2,1)S(1)} dynamic-update-slice(bf16[512,768]{0,1:T(8,128)(2,1)S(1)} %dynamic_update_slice.54, bf16[32,768]{0,1:T(8,128)(2,1)S(1)} %copy.130, s32[]{:T(128)S(6)} %select_n.152, s32[]{:T(128)} %constant.133.clone.1) | dynamic-update-slice | bytes 98308 | tf_op jit(solution)/shard_map/dynamic_update_slice | solution.py:20
  137.0 2.0 %dynamic_update_slice.56 = bf16[512,768]{0,1:T(8,128)(2,1)S(1)} dynamic-update-slice(bf16[512,768]{0,1:T(8,128)(2,1)S(1)} %dynamic_update_slice.55, bf16[32,768]{0,1:T(8,128)(2,1)S(1)} %copy.131, s32[]{:T(128)S(6)} %select_n.154, s32[]{:T(128)} %constant.133.clone.1) | dynamic-update-slice | bytes 98308 | tf_op jit(solution)/shard_map/dynamic_update_slice | solution.py:20
  139.2 2.9 %dynamic_update_slice.57 = bf16[512,768]{0,1:T(8,128)(2,1)S(1)} dynamic-update-slice(bf16[512,768]{0,1:T(8,128)(2,1)S(1)} %dynamic_update_slice.56, bf16[32,768]{0,1:T(8,128)(2,1)S(1)} %copy.132, s32[]{:T(128)S(6)} %select_n.156, s32[]{:T(128)} %constant.133.clone.1) | dynamic-update-slice | bytes 98308 | tf_op jit(solution)/shard_map/dynamic_update_slice | solution.py:20
  142.3 2.9 %dynamic_update_slice.58 = bf16[512,768]{0,1:T(8,128)(2,1)S(1)} dynamic-update-slice(bf16[512,768]{0,1:T(8,128)(2,1)S(1)} %dynamic_update_slice.57, bf16[32,768]{0,1:T(8,128)(2,1)S(1)} %copy.133, s32[]{:T(128)S(6)} %select_n.158, s32[]{:T(128)} %constant.133.clone.1) | dynamic-update-slice | bytes 98308 | tf_op jit(solution)/shard_map/dynamic_update_slice | solution.py:20
  146.1 2.9 %dynamic_update_slice.59 = bf16[512,768]{0,1:T(8,128)(2,1)S(1)} dynamic-update-slice(bf16[512,768]{0,1:T(8,128)(2,1)S(1)} %dynamic_update_slice.58, bf16[32,768]{0,1:T(8,128)(2,1)S(1)} %copy.134, s32[]{:T(128)S(6)} %select_n.160, s32[]{:T(128)} %constant.133.clone.1) | dynamic-update-slice | bytes 98308 | tf_op jit(solution)/shard_map/dynamic_update_slice | solution.py:20
  149.2 2.3 %dynamic_update_slice.60 = bf16[512,768]{0,1:T(8,128)(2,1)S(1)} dynamic-update-slice(bf16[512,768]{0,1:T(8,128)(2,1)S(1)} %dynamic_update_slice.59, bf16[32,768]{0,1:T(8,128)(2,1)S(1)} %copy.135, s32[]{:T(128)S(6)} %select_n.162, s32[]{:T(128)} %constant.133.clone.1) | dynamic-update-slice | bytes 98308 | tf_op jit(solution)/shard_map/dynamic_update_slice | solution.py:20
  151.6 2.9 %dynamic_update_slice.61 = bf16[512,768]{0,1:T(8,128)(2,1)S(1)} dynamic-update-slice(bf16[512,768]{0,1:T(8,128)(2,1)S(1)} %dynamic_update_slice.60, bf16[32,768]{0,1:T(8,128)(2,1)S(1)} %copy.136, s32[]{:T(128)S(6)} %select_n.164, s32[]{:T(128)} %constant.133.clone.1) | dynamic-update-slice | bytes 98308 | tf_op jit(solution)/shard_map/dynamic_update_slice | solution.py:20
  155.4 2.9 %dynamic_update_slice.62 = bf16[512,768]{0,1:T(8,128)(2,1)S(1)} dynamic-update-slice(bf16[512,768]{0,1:T(8,128)(2,1)S(1)} %dynamic_update_slice.61, bf16[32,768]{0,1:T(8,128)(2,1)S(1)} %copy.137, s32[]{:T(128)S(6)} %select_n.166, s32[]{:T(128)} %constant.133.clone.1) | dynamic-update-slice | bytes 98308 | tf_op jit(solution)/shard_map/dynamic_update_slice | solution.py:20
  159.3 2.9 %dynamic_update_slice.63 = bf16[512,768]{0,1:T(8,128)(2,1)S(1)} dynamic-update-slice(bf16[512,768]{0,1:T(8,128)(2,1)S(1)} %dynamic_update_slice.62, bf16[32,768]{0,1:T(8,128)(2,1)S(1)} %copy.138, s32[]{:T(128)S(6)} %select_n.168, s32[]{:T(128)} %constant.133.clone.1) | dynamic-update-slice | bytes 98308 | tf_op jit(solution)/shard_map/dynamic_update_slice | solution.py:20
  162.2 3.3 %fusion.9 = bf16[2,4,64,6,128]{4,2,3,1,0:T(8,128)(2,1)S(1)} fusion(f32[2,4,6,64,128]{4,3,2,1,0:T(8,128)} %fusion.14, bf16[512,6,128,1,1]{0,2,1,4,3:T(8,128)(2,1)S(1)} %bitcast.78, bf16[2,4,6,64,512]{4,3,1,0,2:T(8,128)(2,1)} %get-tuple-element.8, f32[2,4,64,6]{2,3,1,0:T(8,128)S(1)} %copy-done.22, f32[2,4,64,6]{2,3,1,0:T(8,128)S(1)} %copy-done.23), kind=kOutput, calls=%fused_computation.15 | convolution fusion | flops 404226048 | bytes 6316032 | tf_op jit(solution)/shard_map/fnhqk,khd->fnhqd/dot_general | solution.py:106
  166.1 1.8 %reshape.122 = bf16[2,2,2,8,8,768]{5,4,3,2,1,0:T(8,128)(2,1)} reshape(bf16[2,4,64,6,128]{4,3,2,1,0:T(8,128)(2,1)S(1)} %copy.144) | data formatting | bytes 1572864 | tf_op jit(solution)/shard_map/reshape | solution.py:37
  167.9 1.2 copy.145
  169.1 2.5 %convolution_convert_fusion = bf16[512,1536]{1,0:T(8,128)(2,1)} fusion(bf16[512,768]{1,0:T(8,128)(2,1)S(1)} %bitcast.77, bf16[768,1536]{1,0:T(8,128)(2,1)S(1)} %copy-done), kind=kOutput, calls=%fused_computation.12 | convolution fusion | flops 1208745984 | bytes 4718592 | tf_op jit(solution)/shard_map/dot_general | solution.py:116
  (104 shorter events, 9.7 us)
Async XLA Ops:
  0.0 169.1 %copy-start = (bf16[768,1536]{1,0:T(8,128)(2,1)S(1)}, bf16[768,1536]{1,0:T(8,128)(2,1)}, u32[]{:S(2)}) copy-start(bf16[768,1536]{1,0:T(8,128)(2,1)} %param.13) | copy-start | bytes 7077892
  5.6 15.3 %copy-start.1 = (bf16[512,768]{1,0:T(8,128)(2,1)}, bf16[512,768]{1,0:T(8,128)(2,1)S(1)}, u32[]{:S(2)}) copy-start(bf16[512,768]{1,0:T(8,128)(2,1)S(1)} %convolution_convert_fusion.1) | copy-start | bytes 2359300
  5.6 10.8 %copy-start.26 = (f32[1536]{0:T(1024)S(1)}, f32[1536]{0:T(1024)}, u32[]{:S(2)}) copy-start(f32[1536]{0:T(1024)} %param.9) | copy-start | bytes 18436
  9.0 13.5 %copy-start.5 = (bf16[512,1536]{1,0:T(8,128)(2,1)S(1)}, bf16[512,1536]{1,0:T(8,128)(2,1)}, u32[]{:S(2)}) copy-start(bf16[512,1536]{1,0:T(8,128)(2,1)} %param.7) | copy-start | bytes 4718596
  9.1 13.5 %copy-start.25 = (bf16[1536,768]{1,0:T(8,128)(2,1)S(1)}, bf16[1536,768]{1,0:T(8,128)(2,1)}, u32[]{:S(2)}) copy-start(bf16[1536,768]{1,0:T(8,128)(2,1)} %param.10) | copy-start | bytes 7077892
  9.1 7.3 %collective-permute-start = (bf16[32,768]{1,0:T(8,128)(2,1)S(1)}, bf16[32,768]{1,0:T(8,128)(2,1)S(1)}, u32[]{:S(2)}, u32[]{:S(2)}) collective-permute-start(bf16[32,768]{1,0:T(8,128)(2,1)S(1)} %convert_element_type.64), channel_id=1, source_target_pairs={{0,1},{1,2},{2,3},{3,4},{4,5},{5,6},{6,7},{7,8},{8,9},{9,10},{10,1... | collective-permute-start | bytes 147464 | tf_op jit(solution)/shard_map/ppermute | solution.py:19
  16.4 6.2 %collective-permute-start.1 = (bf16[32,768]{1,0:T(8,128)(2,1)S(1)}, bf16[32,768]{1,0:T(8,128)(2,1)S(1)}, u32[]{:S(2)}, u32[]{:S(2)}) collective-permute-start(bf16[32,768]{1,0:T(8,128)(2,1)S(1)} %collective-permute-done), channel_id=1, source_target_pairs={{0,1},{1,2},{2,3},{3,4},{4,5},{5,6},{6,7},{7,8},{8,9},{9,10},{10,1... | collective-permute-start | bytes 147464 | tf_op jit(solution)/shard_map/ppermute | solution.py:19
  22.6 2.4 %copy-start.3 = (bf16[512,768]{1,0:T(8,128)(2,1)S(1)}, bf16[512,768]{1,0:T(8,128)(2,1)}, u32[]{:S(2)}) copy-start(bf16[512,768]{1,0:T(8,128)(2,1)} %convolution_convert_fusion.2) | copy-start | bytes 2359300
  22.6 6.2 %collective-permute-start.2 = (bf16[32,768]{1,0:T(8,128)(2,1)S(1)}, bf16[32,768]{1,0:T(8,128)(2,1)S(1)}, u32[]{:S(2)}, u32[]{:S(2)}) collective-permute-start(bf16[32,768]{1,0:T(8,128)(2,1)S(1)} %collective-permute-done.1), channel_id=1, source_target_pairs={{0,1},{1,2},{2,3},{3,4},{4,5},{5,6},{6,7},{7,8},{8,9},{9,10},{10,1... | collective-permute-start | bytes 147464 | tf_op jit(solution)/shard_map/ppermute | solution.py:19
  25.0 37.8 %copy-start.24 = (s32[32]{0:T(128)S(1)}, s32[32]{0:T(128)}, u32[]{:S(2)}) copy-start(s32[32]{0:T(128)} %param.8) | copy-start | bytes 388
  28.8 6.2 %collective-permute-start.3 = (bf16[32,768]{1,0:T(8,128)(2,1)S(1)}, bf16[32,768]{1,0:T(8,128)(2,1)S(1)}, u32[]{:S(2)}, u32[]{:S(2)}) collective-permute-start(bf16[32,768]{1,0:T(8,128)(2,1)S(1)} %collective-permute-done.2), channel_id=1, source_target_pairs={{0,1},{1,2},{2,3},{3,4},{4,5},{5,6},{6,7},{7,8},{8,9},{9,10},{10,1... | collective-permute-start | bytes 147464 | tf_op jit(solution)/shard_map/ppermute | solution.py:19
  35.0 34.1 %copy-start.6 = (bf16[32,768]{1,0:T(8,128)(2,1)}, bf16[32,768]{1,0:T(8,128)(2,1)S(1)}, u32[]{:S(2)}) copy-start(bf16[32,768]{1,0:T(8,128)(2,1)S(1)} %collective-permute-done.3) | copy-start | bytes 147460
  35.0 21.5 %collective-permute-start.4 = (bf16[32,768]{1,0:T(8,128)(2,1)S(1)}, bf16[32,768]{1,0:T(8,128)(2,1)S(1)}, u32[]{:S(2)}, u32[]{:S(2)}) collective-permute-start(bf16[32,768]{1,0:T(8,128)(2,1)S(1)} %collective-permute-done.3), channel_id=1, source_target_pairs={{0,1},{1,2},{2,3},{3,4},{4,5},{5,6},{6,7},{7,8},{8,9},{9,10},{10,1... | collective-permute-start | bytes 147464 | tf_op jit(solution)/shard_map/ppermute | solution.py:19
  56.6 12.5 %copy-start.7 = (bf16[32,768]{1,0:T(8,128)(2,1)}, bf16[32,768]{1,0:T(8,128)(2,1)S(1)}, u32[]{:S(2)}) copy-start(bf16[32,768]{1,0:T(8,128)(2,1)S(1)} %collective-permute-done.4) | copy-start | bytes 147460
  56.6 6.2 %collective-permute-start.5 = (bf16[32,768]{1,0:T(8,128)(2,1)S(1)}, bf16[32,768]{1,0:T(8,128)(2,1)S(1)}, u32[]{:S(2)}, u32[]{:S(2)}) collective-permute-start(bf16[32,768]{1,0:T(8,128)(2,1)S(1)} %collective-permute-done.4), channel_id=1, source_target_pairs={{0,1},{1,2},{2,3},{3,4},{4,5},{5,6},{6,7},{7,8},{8,9},{9,10},{10,1... | collective-permute-start | bytes 147464 | tf_op jit(solution)/shard_map/ppermute | solution.py:19
  62.8 6.3 %copy-start.8 = (bf16[32,768]{1,0:T(8,128)(2,1)}, bf16[32,768]{1,0:T(8,128)(2,1)S(1)}, u32[]{:S(2)}) copy-start(bf16[32,768]{1,0:T(8,128)(2,1)S(1)} %collective-permute-done.5) | copy-start | bytes 147460
  62.8 6.2 %collective-permute-start.6 = (bf16[32,768]{1,0:T(8,128)(2,1)S(1)}, bf16[32,768]{1,0:T(8,128)(2,1)S(1)}, u32[]{:S(2)}, u32[]{:S(2)}) collective-permute-start(bf16[32,768]{1,0:T(8,128)(2,1)S(1)} %collective-permute-done.5), channel_id=1, source_target_pairs={{0,1},{1,2},{2,3},{3,4},{4,5},{5,6},{6,7},{7,8},{8,9},{9,10},{10,1... | collective-permute-start | bytes 147464 | tf_op jit(solution)/shard_map/ppermute | solution.py:19
  69.0 8.5 %copy-start.9 = (bf16[32,768]{1,0:T(8,128)(2,1)}, bf16[32,768]{1,0:T(8,128)(2,1)S(1)}, u32[]{:S(2)}) copy-start(bf16[32,768]{1,0:T(8,128)(2,1)S(1)} %collective-permute-done.6) | copy-start | bytes 147460
  69.0 6.2 %collective-permute-start.7 = (bf16[32,768]{1,0:T(8,128)(2,1)S(1)}, bf16[32,768]{1,0:T(8,128)(2,1)S(1)}, u32[]{:S(2)}, u32[]{:S(2)}) collective-permute-start(bf16[32,768]{1,0:T(8,128)(2,1)S(1)} %collective-permute-done.6), channel_id=1, source_target_pairs={{0,1},{1,2},{2,3},{3,4},{4,5},{5,6},{6,7},{7,8},{8,9},{9,10},{10,1... | collective-permute-start | bytes 147464 | tf_op jit(solution)/shard_map/ppermute | solution.py:19
  75.2 2.3 %copy-start.11 = (bf16[32,768]{1,0:T(8,128)(2,1)}, bf16[32,768]{1,0:T(8,128)(2,1)S(1)}, u32[]{:S(2)}) copy-start(bf16[32,768]{1,0:T(8,128)(2,1)S(1)} %collective-permute-done.7) | copy-start | bytes 147460
  75.2 6.2 %collective-permute-start.8 = (bf16[32,768]{1,0:T(8,128)(2,1)S(1)}, bf16[32,768]{1,0:T(8,128)(2,1)S(1)}, u32[]{:S(2)}, u32[]{:S(2)}) collective-permute-start(bf16[32,768]{1,0:T(8,128)(2,1)S(1)} %collective-permute-done.7), channel_id=1, source_target_pairs={{0,1},{1,2},{2,3},{3,4},{4,5},{5,6},{6,7},{7,8},{8,9},{9,10},{10,1... | collective-permute-start | bytes 147464 | tf_op jit(solution)/shard_map/ppermute | solution.py:19
  75.2 2.3 %copy-start.4 = (bf16[512,768]{1,0:T(8,128)(2,1)S(1)}, bf16[512,768]{1,0:T(8,128)(2,1)}, u32[]{:S(2)}) copy-start(bf16[512,768]{1,0:T(8,128)(2,1)} %convolution_convert_fusion.2) | copy-start | bytes 2359300
  81.4 15.6 %copy-start.13 = (bf16[32,768]{1,0:T(8,128)(2,1)}, bf16[32,768]{1,0:T(8,128)(2,1)S(1)}, u32[]{:S(2)}) copy-start(bf16[32,768]{1,0:T(8,128)(2,1)S(1)} %collective-permute-done.8) | copy-start | bytes 147460
  81.4 6.2 %collective-permute-start.9 = (bf16[32,768]{1,0:T(8,128)(2,1)S(1)}, bf16[32,768]{1,0:T(8,128)(2,1)S(1)}, u32[]{:S(2)}, u32[]{:S(2)}) collective-permute-start(bf16[32,768]{1,0:T(8,128)(2,1)S(1)} %collective-permute-done.8), channel_id=1, source_target_pairs={{0,1},{1,2},{2,3},{3,4},{4,5},{5,6},{6,7},{7,8},{8,9},{9,10},{10,1... | collective-permute-start | bytes 147464 | tf_op jit(solution)/shard_map/ppermute | solution.py:19
  87.6 9.4 %copy-start.15 = (bf16[32,768]{1,0:T(8,128)(2,1)}, bf16[32,768]{1,0:T(8,128)(2,1)S(1)}, u32[]{:S(2)}) copy-start(bf16[32,768]{1,0:T(8,128)(2,1)S(1)} %collective-permute-done.9) | copy-start | bytes 147460
  87.6 6.2 %collective-permute-start.10 = (bf16[32,768]{1,0:T(8,128)(2,1)S(1)}, bf16[32,768]{1,0:T(8,128)(2,1)S(1)}, u32[]{:S(2)}, u32[]{:S(2)}) collective-permute-start(bf16[32,768]{1,0:T(8,128)(2,1)S(1)} %collective-permute-done.9), channel_id=1, source_target_pairs={{0,1},{1,2},{2,3},{3,4},{4,5},{5,6},{6,7},{7,8},{8,9},{9,10},{10,1... | collective-permute-start | bytes 147464 | tf_op jit(solution)/shard_map/ppermute | solution.py:19
  93.8 3.1 %copy-start.17 = (bf16[32,768]{1,0:T(8,128)(2,1)}, bf16[32,768]{1,0:T(8,128)(2,1)S(1)}, u32[]{:S(2)}) copy-start(bf16[32,768]{1,0:T(8,128)(2,1)S(1)} %collective-permute-done.10) | copy-start | bytes 147460
  93.8 6.2 %collective-permute-start.11 = (bf16[32,768]{1,0:T(8,128)(2,1)S(1)}, bf16[32,768]{1,0:T(8,128)(2,1)S(1)}, u32[]{:S(2)}, u32[]{:S(2)}) collective-permute-start(bf16[32,768]{1,0:T(8,128)(2,1)S(1)} %collective-permute-done.10), channel_id=1, source_target_pairs={{0,1},{1,2},{2,3},{3,4},{4,5},{5,6},{6,7},{7,8},{8,9},{9,10},{10,1... | collective-permute-start | bytes 147464 | tf_op jit(solution)/shard_map/ppermute | solution.py:19
  93.8 3.2 %copy-start.2 = (bf16[512,768]{1,0:T(8,128)(2,1)S(1)}, bf16[512,768]{1,0:T(8,128)(2,1)}, u32[]{:S(2)}) copy-start(bf16[512,768]{1,0:T(8,128)(2,1)} %copy-done.1) | copy-start | bytes 2359300
  100.1 6.6 %copy-start.18 = (bf16[32,768]{1,0:T(8,128)(2,1)}, bf16[32,768]{1,0:T(8,128)(2,1)S(1)}, u32[]{:S(2)}) copy-start(bf16[32,768]{1,0:T(8,128)(2,1)S(1)} %collective-permute-done.11) | copy-start | bytes 147460
  100.1 6.2 %collective-permute-start.12 = (bf16[32,768]{1,0:T(8,128)(2,1)S(1)}, bf16[32,768]{1,0:T(8,128)(2,1)S(1)}, u32[]{:S(2)}, u32[]{:S(2)}) collective-permute-start(bf16[32,768]{1,0:T(8,128)(2,1)S(1)} %collective-permute-done.11), channel_id=1, source_target_pairs={{0,1},{1,2},{2,3},{3,4},{4,5},{5,6},{6,7},{7,8},{8,9},{9,10},{10,1... | collective-permute-start | bytes 147464 | tf_op jit(solution)/shard_map/ppermute | solution.py:19
  106.3 6.3 %copy-start.20 = (bf16[32,768]{1,0:T(8,128)(2,1)}, bf16[32,768]{1,0:T(8,128)(2,1)S(1)}, u32[]{:S(2)}) copy-start(bf16[32,768]{1,0:T(8,128)(2,1)S(1)} %collective-permute-done.12) | copy-start | bytes 147460
  106.3 6.3 %collective-permute-start.13 = (bf16[32,768]{1,0:T(8,128)(2,1)S(1)}, bf16[32,768]{1,0:T(8,128)(2,1)}, u32[]{:S(2)}, u32[]{:S(2)}) collective-permute-start(bf16[32,768]{1,0:T(8,128)(2,1)S(1)} %collective-permute-done.12), channel_id=1, source_target_pairs={{0,1},{1,2},{2,3},{3,4},{4,5},{5,6},{6,7},{7,8},{8,9},{9,10},{10,1... | collective-permute-start | bytes 147464 | tf_op jit(solution)/shard_map/ppermute | solution.py:19
  112.6 45.7 %collective-permute-start.14 = (bf16[32,768]{1,0:T(8,128)(2,1)}, bf16[32,768]{1,0:T(8,128)(2,1)}, u32[]{:S(2)}, u32[]{:S(2)}) collective-permute-start(bf16[32,768]{1,0:T(8,128)(2,1)} %collective-permute-done.13), channel_id=1, source_target_pairs={{0,1},{1,2},{2,3},{3,4},{4,5},{5,6},{6,7},{7,8},{8,9},{9,10},{10,1... | collective-permute-start | bytes 147464 | tf_op jit(solution)/shard_map/ppermute | solution.py:19
  113.5 20.3 %copy-start.10 = (bf16[32,768]{1,0:T(8,128)(2,1)S(1)}, bf16[32,768]{1,0:T(8,128)(2,1)}, u32[]{:S(2)}) copy-start(bf16[32,768]{1,0:T(8,128)(2,1)} %copy-done.9) | copy-start | bytes 147460
  116.0 20.9 %copy-start.12 = (bf16[32,768]{1,0:T(8,128)(2,1)S(1)}, bf16[32,768]{1,0:T(8,128)(2,1)}, u32[]{:S(2)}) copy-start(bf16[32,768]{1,0:T(8,128)(2,1)} %copy-done.11) | copy-start | bytes 147460
  118.5 20.5 %copy-start.14 = (bf16[32,768]{1,0:T(8,128)(2,1)S(1)}, bf16[32,768]{1,0:T(8,128)(2,1)}, u32[]{:S(2)}) copy-start(bf16[32,768]{1,0:T(8,128)(2,1)} %copy-done.13) | copy-start | bytes 147460
  121.1 21.0 %copy-start.16 = (bf16[32,768]{1,0:T(8,128)(2,1)S(1)}, bf16[32,768]{1,0:T(8,128)(2,1)}, u32[]{:S(2)}) copy-start(bf16[32,768]{1,0:T(8,128)(2,1)} %copy-done.15) | copy-start | bytes 147460
  133.9 15.1 %copy-start.19 = (bf16[32,768]{1,0:T(8,128)(2,1)S(1)}, bf16[32,768]{1,0:T(8,128)(2,1)}, u32[]{:S(2)}) copy-start(bf16[32,768]{1,0:T(8,128)(2,1)} %copy-done.18) | copy-start | bytes 147460
  137.0 14.4 %copy-start.21 = (bf16[32,768]{1,0:T(8,128)(2,1)S(1)}, bf16[32,768]{1,0:T(8,128)(2,1)}, u32[]{:S(2)}) copy-start(bf16[32,768]{1,0:T(8,128)(2,1)} %copy-done.20) | copy-start | bytes 147460
  139.2 22.9 %copy-start.22 = (f32[2,4,64,6]{2,3,1,0:T(8,128)S(1)}, f32[2,4,64,6]{2,3,1,0:T(8,128)}, u32[]{:S(2)}) copy-start(f32[2,4,64,6]{2,3,1,0:T(8,128)} %get-tuple-element.5) | copy-start | bytes 36868
  142.3 19.9 %copy-start.23 = (f32[2,4,64,6]{2,3,1,0:T(8,128)S(1)}, f32[2,4,64,6]{2,3,1,0:T(8,128)}, u32[]{:S(2)}) copy-start(f32[2,4,64,6]{2,3,1,0:T(8,128)} %get-tuple-element.6) | copy-start | bytes 36868
